TPU v7x, 32 devices: a whole 2x2x4 slice. The times are simulated.
32 devices in a mesh: sec: 2 (over core), var: 4 (over z), trait: 4 (over y, x).
Axes of the slice: x: 2, y: 2, z: 4, core: 2. Of those that a mesh axis runs over, the one named last changes fastest.
Arguments:
- z_typed: bfloat16 [32768, 512], P(('sec', 'var'), 'trait'), may hold values from -6 to 6
- band_inverse: bfloat16 [256, 128, 384], P(('sec', 'var')), may hold values from -0.3125 to 0.3125
- ld_untyped: bfloat16 [512, 128, 512], P(('sec', 'var')), may hold values from -0.375 to 0.375
- trait_mix: bfloat16 [512, 512], replicated, may hold values from -0.25 to 0.25
- win_start: int32 [512], P(('sec', 'var')), may hold values from 0 to 255, as said below
- win_count: int32 [512], P(('sec', 'var')), may hold values from 1 to 4, as said below
Outputs:
- imputed_mixed: bfloat16 [65536, 512], P(('sec', 'var'), 'trait')
Inputs may be any that keep to these rules, and one draw needn't show every extreme that they name: Windows follow chromosome order: within the 64 untyped blocks of one index g of sec+var, win_start never falls, and every window lies in typed blocks g * 32 - 32 to (g + 1) * 32 + 31; the first window of each index starts at its lower end (or at 0) and the last one ends at its upper end (or at the chromosome's end). win_start + win_count never exceeds 256.
All inputs are finite; a program needn't handle non-finite values.
Results may differ from a plain program's by a relative error of at most 0.0057.
Values may be sent and summed in bfloat16 or wider, within the bound.
A program may use at most 64 MiB of HBM per device.

v0:
```python
import functools

import jax
import jax.numpy as jnp
from jax import lax
from jax.experimental import pallas as pl
from jax.experimental.pallas import tpu as pltpu
from jax.sharding import PartitionSpec as P

BLK = 128
WIN = 4
HEAD_SIZES = ()
CHUNK_BLOCKS = 4
LAST_BLOCKS = 2
AHEAD = 2
LAG = 1
UNTYPED_TILE = 32
MESH = pl.DeviceIdType.MESH


def chunk_plan(blocks):
    plan = []
    at = LAST_BLOCKS
    sizes = list(HEAD_SIZES)
    while at < blocks:
        size = min(sizes.pop(0) if sizes else CHUNK_BLOCKS, blocks - at)
        plan.append((at, size))
        at += size
    plan.append((0, LAST_BLOCKS))
    return plan


def mixed_kernel(
    plan, blocks, groups, var_size,
    z_ref, band_ref, mix_ref, ld_ref, ext_ref, ldv_ref,
    zb, bandv, w, gathered, mv, results, mx,
    z_sem, ld_sem, band_sem, mix_sem, own_sem, edge_send, edge_recv, in_send, in_recv, out_send, out_recv, halo_send, halo_recv,
):
    t = lax.axis_index("trait")
    g = lax.axis_index("sec") * var_size + lax.axis_index("var")
    x_peer = t + 1 - 2 * lax.rem(t, 2)
    y_peer = t + 2 - 4 * (t // 2)
    far_peer = x_peer + y_peer - t
    peers = (t, x_peer, y_peer, far_peer)
    others = range(1, len(peers))
    right = {"sec": (g + 1) // var_size, "var": lax.rem(g + 1, var_size)}
    left_g = lax.rem(g + groups - 1, groups)
    left = {"sec": left_g // var_size, "var": lax.rem(left_g, var_size)}
    has_left, has_right = g > 0, g < groups - 1
    rows = blocks * BLK
    order = range(len(plan))

    def rows_of(c, offset=0):
        return pl.ds(offset + plan[c][0] * BLK, plan[c][1] * BLK)

    barrier = pltpu.get_barrier_semaphore()

    def greet(device):
        pl.semaphore_signal(barrier, inc=1, device_id=device, device_id_type=MESH)

    for j in others:
        greet({"trait": peers[j]})
    pl.when(has_left)(lambda: greet(left))
    pl.when(has_right)(lambda: greet(right))

    def remote(src, dst, send, recv, device):
        return pltpu.make_async_remote_copy(
            src_ref=src, dst_ref=dst, send_sem=send, recv_sem=recv,
            device_id=device, device_id_type=MESH,
        )

    load_z = pltpu.make_async_copy(z_ref, zb.at[pl.ds(BLK, rows)], z_sem)
    load_z.start()
    def load_band(c):
        part = pl.ds(*plan[c])
        return pltpu.make_async_copy(band_ref.at[part], bandv.at[part], band_sem.at[c])

    for c in order:
        load_band(c).start()
    load_mix = [
        pltpu.make_async_copy(
            mix_ref.at[
                pl.ds(pl.multiple_of(taken * BLK, BLK), BLK), pl.ds(pl.multiple_of(given * BLK, BLK), BLK)
            ],
            mv.at[pl.ds(i * BLK, BLK), pl.ds(j * BLK, BLK)],
            mix_sem.at[i, j],
        )
        for i, taken in enumerate(peers)
        for j, given in enumerate(peers)
    ]
    for copy in load_mix:
        copy.start()
    load_ld = pltpu.make_async_copy(ld_ref, ldv_ref, ld_sem)

    @pl.when(jnp.logical_not(has_left))
    def _():
        zb[pl.ds(0, BLK), :] = jnp.zeros((BLK, BLK), zb.dtype)

    @pl.when(jnp.logical_not(has_right))
    def _():
        zb[pl.ds(rows + BLK, BLK), :] = jnp.zeros((BLK, BLK), zb.dtype)

    edge_right = remote(
        z_ref.at[pl.ds(rows - BLK, BLK)], zb.at[pl.ds(0, BLK)], edge_send.at[0], edge_recv.at[0], right
    )
    edge_left = remote(
        z_ref.at[pl.ds(0, BLK)], zb.at[pl.ds(rows + BLK, BLK)], edge_send.at[1], edge_recv.at[1], left
    )

    def whiten(c):
        load_band(c).wait()
        if sum(plan[c]) == blocks:
            pl.when(has_right)(edge_left.wait_recv)
        if plan[c][0] == 0:
            pl.when(has_left)(edge_right.wait_recv)

        def one(i, carry):
            b = plan[c][0] + i
            first = pl.multiple_of(b * BLK, BLK)
            sums = jnp.dot(bandv[b], zb[pl.ds(first, 3 * BLK), :], preferred_element_type=jnp.float32)
            w[pl.ds(first, BLK), :] = sums.astype(w.dtype)
            return carry

        lax.fori_loop(0, plan[c][1], one, 0, unroll=True)

    def part_of(c, peer):
        part = plan[c][1] * BLK // len(peers)
        return pl.ds(pl.multiple_of(plan[c][0] * BLK + peer * part, part), part)

    def share_of(c):
        return pl.ds(plan[c][0] * BLK // len(peers), plan[c][1] * BLK // len(peers))

    def sends_in(c):
        return [
            remote(
                w.at[part_of(c, peers[j])], gathered.at[j - 1, share_of(c)],
                in_send.at[j - 1, c], in_recv.at[j - 1, c], {"trait": peers[j]},
            )
            for j in others
        ]

    def sends_out(c):
        return [
            remote(
                results.at[j - 1, share_of(c)], mx.at[part_of(c, t)],
                out_send.at[j - 1, c], out_recv.at[j - 1, c], {"trait": peers[j]},
            )
            for j in others
        ]

    def arrivals(c):
        return [
            remote(
                results.at[j - 1, share_of(c)], mx.at[part_of(c, peers[j])],
                out_send.at[j - 1, c], out_recv.at[j - 1, c], {"trait": peers[j]},
            )
            for j in others
        ]

    def halos(c, j):
        part = plan[c][1] * BLK // len(peers)
        above = pl.ds(pl.multiple_of(2 * rows + plan[c][0] * BLK + peers[j] * part, part), part)
        mine = part_of(c, peers[j])
        return (
            remote(mx.at[mine], ext_ref.at[mine], halo_send.at[0, j, c], halo_recv.at[0, j, c], right),
            remote(mx.at[mine], ext_ref.at[above], halo_send.at[1, j, c], halo_recv.at[1, j, c], left),
        )

    def send_halos(c, j):
        to_right, to_left = halos(c, j)
        pl.when(has_right)(to_right.start)
        pl.when(has_left)(to_left.start)

    def keep(c):
        return pltpu.make_async_copy(
            mx.at[rows_of(c)], ext_ref.at[rows_of(c, rows)], own_sem.at[c]
        )

    def mix(c):
        all_traits = jnp.concatenate(
            [w[part_of(c, t), :]] + [gathered[j - 1, share_of(c), :] for j in others], axis=1
        )
        sums = jnp.dot(all_traits, mv[...], preferred_element_type=jnp.float32).astype(mx.dtype)
        mx[part_of(c, t), :] = sums[:, :BLK]
        for j in others:
            results[j - 1, share_of(c), :] = sums[:, j * BLK : (j + 1) * BLK]

    load_z.wait()
    for c in order[: AHEAD + 1]:
        whiten(c)
    pl.semaphore_wait(barrier, len(others) + has_left.astype(jnp.int32) + has_right.astype(jnp.int32))
    pl.when(has_right)(edge_right.start)
    pl.when(has_left)(edge_left.start)
    for c in order[:AHEAD]:
        for copy in sends_in(c):
            copy.start()
    load_ld.start()
    for copy in load_mix:
        copy.wait()
    chunks = len(plan)
    for i in range(chunks + LAG):
        if i < chunks:
            for copy in sends_in(i):
                copy.wait_recv()
            mix(i)
            for copy in sends_out(i):
                copy.start()
            send_halos(i, 0)
        if i + AHEAD < chunks:
            for copy in sends_in(i + AHEAD):
                copy.start()
        if i >= LAG:
            c = i - LAG
            for j, copy in zip(others, arrivals(c)):
                copy.wait_recv()
                send_halos(c, j)
            keep(c).start()
        if i + AHEAD + 1 < chunks:
            whiten(i + AHEAD + 1)
    for c in order:
        for copy in sends_in(c) + sends_out(c):
            copy.wait_send()
        keep(c).wait()
        every = [halos(c, j) for j in range(len(peers))]

        @pl.when(has_right)
        def _():
            for to_right, to_left in every:
                to_right.wait_send()
                to_left.wait_recv()

        @pl.when(has_left)
        def _():
            for to_right, to_left in every:
                to_left.wait_send()
                to_right.wait_recv()

    load_ld.wait()
    pl.when(has_right)(edge_right.wait_send)
    pl.when(has_left)(edge_left.wait_send)


def mixed_with_neighbours(z_typed, band_inverse, trait_mix, ld_untyped, groups, var_size):
    rows = z_typed.shape[0]
    blocks = rows // BLK
    plan = chunk_plan(blocks)
    peers = trait_mix.shape[0] // BLK
    chunks = len(plan)
    dma = pltpu.SemaphoreType.DMA
    kind = z_typed.dtype
    return pl.pallas_call(
        functools.partial(mixed_kernel, plan, blocks, groups, var_size),
        out_shape=(pltpu.VMEM((3 * rows, BLK), kind), pltpu.VMEM(ld_untyped.shape, kind)),
        in_specs=[pl.BlockSpec(memory_space=pl.ANY)] * 4,
        out_specs=(pl.BlockSpec(memory_space=pl.ANY),) * 2,
        scratch_shapes=[
            pltpu.VMEM((rows + 2 * BLK, BLK), kind),
            pltpu.VMEM(band_inverse.shape, kind),
            pltpu.VMEM((rows, BLK), kind),
            pltpu.VMEM((peers - 1, rows // peers, BLK), kind),
            pltpu.VMEM(trait_mix.shape, kind),
            pltpu.VMEM((peers - 1, rows // peers, BLK), kind),
            pltpu.VMEM((rows, BLK), kind),
            dma, dma, dma((chunks,)), dma((peers, peers)), dma((chunks,)),
            dma((2,)), dma((2,)),
            dma((peers - 1, chunks)), dma((peers - 1, chunks)),
            dma((peers - 1, chunks)), dma((peers - 1, chunks)),
            dma((2, peers, chunks)), dma((2, peers, chunks)),
        ],
        compiler_params=pltpu.CompilerParams(
            collective_id=0, has_side_effects=True, vmem_limit_bytes=16 * 1024 * 1024
        ),
        name="mixed_kernel",
    )(*(pltpu.with_memory_space_constraint(v, pltpu.HBM) for v in (z_typed, band_inverse, trait_mix, ld_untyped)))


def impute_kernel(blocks, var_size, start_ref, count_ref, ext_ref, ld_ref, out_ref):
    g = lax.axis_index("sec") * var_size + lax.axis_index("var")
    tile = out_ref.shape[0]
    first = pl.program_id(0) * tile
    for i in range(tile):
        start = start_ref[first + i] - (g - 1) * blocks
        count = count_ref[first + i]
        parts = []
        for s in range(WIN):
            block = ext_ref[jnp.clip(start + s, 0, 3 * blocks - 1)]
            parts.append(jnp.where(s < count, block, jnp.zeros_like(block)))
        window = jnp.concatenate(parts, axis=0)
        sums = jnp.dot(ld_ref[first + i], window, preferred_element_type=jnp.float32)
        out_ref[i] = sums.astype(out_ref.dtype)


def impute(ext, ld_untyped, win_start, win_count, var_size):
    untyped = ld_untyped.shape[0]
    total = ext.shape[0] // BLK
    cols = ext.shape[1]
    return pl.pallas_call(
        functools.partial(impute_kernel, total // 3, var_size),
        grid_spec=pltpu.PrefetchScalarGridSpec(
            num_scalar_prefetch=2,
            grid=(untyped // UNTYPED_TILE,),
            in_specs=[
                pl.BlockSpec(memory_space=pltpu.VMEM),
                pl.BlockSpec(memory_space=pltpu.VMEM),
            ],
            out_specs=pl.BlockSpec((UNTYPED_TILE, BLK, cols), lambda i, *_: (i, 0, 0)),
        ),
        out_shape=jax.ShapeDtypeStruct((untyped, BLK, cols), ext.dtype),
        compiler_params=pltpu.CompilerParams(vmem_limit_bytes=24 * 1024 * 1024),
        name="impute_kernel",
    )(win_start, win_count, ext.reshape(total, BLK, cols), ld_untyped)


def on_device(groups, var_size, z_typed, band_inverse, ld_untyped, trait_mix, win_start, win_count):
    ext, ld_near = mixed_with_neighbours(z_typed, band_inverse, trait_mix, ld_untyped, groups, var_size)
    imputed = impute(ext, ld_near, win_start, win_count, var_size)
    return imputed.reshape(ld_untyped.shape[0] * BLK, z_typed.shape[1])


def solution(mesh):
    var_size = mesh.shape["var"]
    groups = mesh.shape["sec"] * var_size
    in_specs = (
        P(("sec", "var"), "trait"),
        P(("sec", "var"), None, None),
        P(("sec", "var"), None, None),
        P(),
        P(("sec", "var")),
        P(("sec", "var")),
    )
    return jax.shard_map(
        functools.partial(on_device, groups, var_size),
        mesh=mesh, in_specs=in_specs, out_specs=P(("sec", "var"), "trait"), check_vma=False,
    )
```

profile of v0, /device:TPU:1, one launch (start us, length us, event | category | flops | bytes accessed | tf_op | source)
XLA Modules:
  0.0 54.0 jit_solution(11449306717417890636)
XLA Ops:
  0.0 0.0 copy-start.1
  0.0 0.0 copy-start
  0.0 49.9 %mixed_kernel.1 = (bf16[12288,128]{1,0:T(8,128)(2,1)S(1)}, bf16[64,128,512]{2,1,0:T(8,128)(2,1)S(1)}) custom-call(bf16[4096,128]{1,0:T(8,128)(2,1)} %z_ref.1, bf16[32,128,384]{2,1,0:T(8,128)(2,1)} %band_ref.1, bf16[512,512]{1,0:T(8,128)(2,1)} %mix_ref.1, bf16[64,128,512]{2,1,0:T(8,128)(2,1)} %ld_ref.1), custom_call_target="tpu_custom_call" | custom-call | tf_op jit(solution)/shard_map/mixed_kernel/pallas_call | solution.py:251
  49.9 0.0 copy-done.1
  49.9 0.0 copy-done
  49.9 4.1 %impute_kernel.1 = bf16[64,128,128]{2,1,0:T(8,128)(2,1)} custom-call(s32[64]{0:T(128)S(1)} %copy-done, s32[64]{0:T(128)S(1)} %copy-done.1, bf16[96,128,128]{2,1,0:T(8,128)(2,1)S(1)} %bitcast.2, bf16[64,128,512]{2,1,0:T(8,128)(2,1)S(1)} %get-tuple-element.8.ld_ref), custom_call_target="tpu_custom_call" | custom-call | tf_op jit(solution)/shard_map/impute_kernel/pallas_call | solution.py:297
Async XLA Ops:
  0.0 49.9 %copy-start.1 = (s32[64]{0:T(128)S(1)}, s32[64]{0:T(128)}, u32[]{:S(2)}) copy-start(s32[64]{0:T(128)} %count_ref.1) | copy-start | bytes 772
  0.0 49.9 %copy-start = (s32[64]{0:T(128)S(1)}, s32[64]{0:T(128)}, u32[]{:S(2)}) copy-start(s32[64]{0:T(128)} %start_ref.1) | copy-start | bytes 772
where the time goes:
time: 54.2 us; the launch traced here: 54 us
  Pallas kernels  54 us (100%)
    pallas_call x1, Pallas kernels, mixed_with_neighbours(): pl.pallas_call(functools.partial(mixed_kernel, plan, blocks, groups, var_...  49.9 us
    pallas_call x1, Pallas kernels, impute(): pl.pallas_call(functools.partial(impute_kernel, total // 3, var_size), gr...  4.09 us

commit v1 on v0

v1 whole, which is shorter than its diff:
```python
import functools

import jax
import jax.numpy as jnp
from jax import lax
from jax.experimental import pallas as pl
from jax.experimental.pallas import tpu as pltpu
from jax.sharding import PartitionSpec as P

BLK = 128
WIN = 4
LATE = 4
SHIFT = LATE - 1
FIRST = 4
CHUNK = 4
AHEAD = 2
LAG = 1
BY_PARTS = 1
FOREIGN_AT = 5
GROUP = 8
MESH = pl.DeviceIdType.MESH


def chunk_plan(blocks):
    first = blocks // 2 - FIRST // 2
    starts = []
    at = LATE
    while at < blocks - LATE:
        if at == first:
            at += FIRST
            continue
        stop = first if at < first else blocks - LATE
        starts.append((at, min(CHUNK, stop - at)))
        at += starts[-1][1]
    return (first, FIRST), starts + [(0, LATE), (blocks - LATE, LATE)]


def job_list(blocks):
    first, chunks = chunk_plan(blocks)
    rows = blocks * BLK
    own = [("own", start, size, start * BLK, blocks + start - SHIFT) for start, size in chunks]
    extra = [
        ("left", first[0], first[1], rows, first[0] - SHIFT),
        ("right", first[0], first[1], rows + FIRST * BLK, 2 * blocks + first[0] - SHIFT),
        ("first", first[0], first[1], first[0] * BLK, blocks + first[0] - SHIFT),
    ]
    return own[:FOREIGN_AT] + extra + own[FOREIGN_AT:]


def mixed_kernel(
    jobs, blocks, groups, var_size,
    z_ref, band_ref, mix_ref, ld_ref, start_ref, count_ref, ext_ref, late_ref, ldv_ref, part_ref,
    zb, bandv, w, gathered, mv, results, starts, counts,
    z_sem, ld_sem, win_sem, band_sem, mix_sem, edge_send, edge_recv, in_send, in_recv, out_send, out_recv,
    first_send, first_recv, halo_send, halo_recv,
):
    t = lax.axis_index("trait")
    g = lax.axis_index("sec") * var_size + lax.axis_index("var")
    x_peer = t + 1 - 2 * lax.rem(t, 2)
    y_peer = t + 2 - 4 * (t // 2)
    far_peer = x_peer + y_peer - t
    peers = (t, x_peer, y_peer, far_peer)
    others = range(1, len(peers))
    right = {"sec": (g + 1) // var_size, "var": lax.rem(g + 1, var_size)}
    left_g = lax.rem(g + groups - 1, groups)
    left = {"sec": left_g // var_size, "var": lax.rem(left_g, var_size)}
    has_left, has_right = g > 0, g < groups - 1
    rows = blocks * BLK
    count_jobs = len(jobs)
    order = range(count_jobs)
    first_c = [c for c in order if jobs[c][0] == "first"][0]

    barrier = pltpu.get_barrier_semaphore()

    def greet(device):
        pl.semaphore_signal(barrier, inc=1, device_id=device, device_id_type=MESH)

    for j in others:
        greet({"trait": peers[j]})
    pl.when(has_left)(lambda: greet(left))
    pl.when(has_right)(lambda: greet(right))

    def remote(src, dst, send, recv, device):
        return pltpu.make_async_remote_copy(
            src_ref=src, dst_ref=dst, send_sem=send, recv_sem=recv,
            device_id=device, device_id_type=MESH,
        )

    def gated(c, act):
        kind = jobs[c][0]
        if kind == "left":
            pl.when(has_left)(act)
        elif kind == "right":
            pl.when(has_right)(act)
        else:
            act()

    def is_own(c):
        return jobs[c][0] in ("own", "first")

    load_z = pltpu.make_async_copy(z_ref, zb.at[pl.ds(BLK, rows)], z_sem)
    load_z.start()

    def load_band(c):
        part = pl.ds(jobs[c][1], jobs[c][2])
        return pltpu.make_async_copy(band_ref.at[part], bandv.at[part], band_sem.at[c])

    to_whiten = [first_c] + [c for c in order if jobs[c][0] == "own"]
    for c in to_whiten:
        load_band(c).start()
    load_mix = [
        pltpu.make_async_copy(
            mix_ref.at[
                pl.ds(pl.multiple_of(taken * BLK, BLK), BLK), pl.ds(pl.multiple_of(given * BLK, BLK), BLK)
            ],
            mv.at[pl.ds(i * BLK, BLK), pl.ds(j * BLK, BLK)],
            mix_sem.at[i, j],
        )
        for i, taken in enumerate(peers)
        for j, given in enumerate(peers)
    ]
    for copy in load_mix:
        copy.start()
    load_ld = pltpu.make_async_copy(ld_ref, ldv_ref, ld_sem)
    load_windows = [
        pltpu.make_async_copy(start_ref, starts, win_sem.at[0]),
        pltpu.make_async_copy(count_ref, counts, win_sem.at[1]),
    ]

    @pl.when(jnp.logical_not(has_left))
    def _():
        zb[pl.ds(0, BLK), :] = jnp.zeros((BLK, BLK), zb.dtype)

    @pl.when(jnp.logical_not(has_right))
    def _():
        zb[pl.ds(rows + BLK, BLK), :] = jnp.zeros((BLK, BLK), zb.dtype)

    edge_right = remote(
        z_ref.at[pl.ds(rows - BLK, BLK)], zb.at[pl.ds(0, BLK)], edge_send.at[0], edge_recv.at[0], right
    )
    edge_left = remote(
        z_ref.at[pl.ds(0, BLK)], zb.at[pl.ds(rows + BLK, BLK)], edge_send.at[1], edge_recv.at[1], left
    )

    def whiten(c):
        _, start, size, _, _ = jobs[c]
        load_band(c).wait()
        if start + size == blocks:
            pl.when(has_right)(edge_left.wait_recv)
        if start == 0:
            pl.when(has_left)(edge_right.wait_recv)

        def one(i, carry):
            b = start + i
            row = pl.multiple_of(b * BLK, BLK)
            sums = jnp.dot(bandv[b], zb[pl.ds(row, 3 * BLK), :], preferred_element_type=jnp.float32)
            w[pl.ds(row, BLK), :] = sums.astype(w.dtype)
            return carry

        lax.fori_loop(0, size, one, 0, unroll=True)

    first_at = pl.ds(jobs[first_c][3], FIRST * BLK)
    first_right = remote(
        w.at[first_at], w.at[pl.ds(rows, FIRST * BLK)], first_send.at[0], first_recv.at[0], right
    )
    first_left = remote(
        w.at[first_at], w.at[pl.ds(rows + FIRST * BLK, FIRST * BLK)], first_send.at[1], first_recv.at[1], left
    )

    def part_rows(c):
        return jobs[c][2] * BLK // len(peers)

    def part_of(c, peer):
        part = part_rows(c)
        return pl.ds(pl.multiple_of(jobs[c][3] + peer * part, part), part)

    def land_of(c, peer):
        part = part_rows(c)
        if part % BLK == 0:
            return ext_ref.at[jobs[c][4] + peer]
        row = peer * part
        return ext_ref.at[jobs[c][4] + row // BLK, pl.ds(pl.multiple_of(lax.rem(row, BLK), part), part)]

    def share_of(c):
        return pl.ds(jobs[c][3] // len(peers), part_rows(c))

    def sends_in(c):
        return [
            remote(
                w.at[part_of(c, peers[j])], gathered.at[j - 1, share_of(c)],
                in_send.at[j - 1, c], in_recv.at[j - 1, c], {"trait": peers[j]},
            )
            for j in others
        ]

    def sends_out(c):
        return [
            remote(
                results.at[j - 1, share_of(c)], land_of(c, t),
                out_send.at[j - 1, c], out_recv.at[j - 1, c], {"trait": peers[j]},
            )
            for j in others
        ]

    def arrivals(c):
        return [
            remote(
                results.at[j - 1, share_of(c)], land_of(c, peers[j]),
                out_send.at[j - 1, c], out_recv.at[j - 1, c], {"trait": peers[j]},
            )
            for j in others
        ]

    def start_in(c):
        def act():
            if jobs[c][0] == "left":
                first_right.wait_recv()
            if jobs[c][0] == "right":
                first_left.wait_recv()
            for copy in sends_in(c):
                copy.start()

        gated(c, act)

    def mix(c):
        def act():
            for copy in sends_in(c):
                copy.wait_recv()
            all_traits = jnp.concatenate(
                [w[part_of(c, t), :]] + [gathered[j - 1, share_of(c), :] for j in others], axis=1
            )
            sums = jnp.dot(all_traits, mv[...], preferred_element_type=jnp.float32).astype(w.dtype)
            land_of(c, t)[...] = sums[:, :BLK]
            for j in others:
                results[j - 1, share_of(c), :] = sums[:, j * BLK : (j + 1) * BLK]
            for copy in sends_out(c):
                copy.start()

        gated(c, act)

    def halo(c, side, offset, length, slot):
        _, start, size, _, land = jobs[c]
        if side == 0:
            place, at = (late_ref, start) if start < LATE else (ext_ref, start - SHIFT)
        elif start >= blocks - LATE:
            place, at = late_ref, 2 * LATE + start - blocks
        else:
            place, at = ext_ref, 2 * blocks + start - SHIFT
        return remote(
            ext_ref.at[pl.ds(land + offset, length)], place.at[pl.ds(at + offset, length)],
            halo_send.at[side, slot, c], halo_recv.at[side, slot, c], right if side == 0 else left,
        )

    own_jobs = [c for c in order if jobs[c][0] == "own"]
    by_parts = own_jobs[:BY_PARTS]
    tails = own_jobs[-2:]

    def piece(c, side, j):
        return halo(c, side, peers[j], 1, j)

    def pieces(c, side):
        if c in by_parts:
            return [piece(c, side, j) for j in range(len(peers))]
        return [halo(c, side, 0, jobs[c][2], 0)]

    def is_late(c, side):
        return (side == 0 and jobs[c][1] < LATE) or (side == 1 and jobs[c][1] >= blocks - LATE)

    def send_halo(c, side):
        for copy in pieces(c, side):
            pl.when(has_right if side == 0 else has_left)(copy.start)

    near = 3 * blocks - 2 * LATE
    for b in (0, near + 1):
        ext_ref[b] = jnp.zeros((BLK, BLK), ext_ref.dtype)
    load_z.wait()
    whiten(first_c)
    pending = [c for c in to_whiten if c != first_c]

    def whiten_upto(i):
        if i < count_jobs and jobs[i][0] == "own" and i in pending:
            pending.remove(i)
            whiten(i)

    for i in range(AHEAD):
        whiten_upto(i)
    pl.semaphore_wait(barrier, len(others) + has_left.astype(jnp.int32) + has_right.astype(jnp.int32))
    pl.when(has_right)(first_right.start)
    pl.when(has_left)(first_left.start)
    for c in order[:AHEAD]:
        start_in(c)
    pl.when(has_right)(edge_right.start)
    pl.when(has_left)(edge_left.start)
    load_ld.start()
    for copy in load_windows:
        copy.start()
    whiten_upto(AHEAD)
    for copy in load_mix:
        copy.wait()

    def settle(c):
        def act():
            for j, copy in zip(others, arrivals(c)):
                copy.wait_recv()
                if c in by_parts:
                    pl.when(has_right)(piece(c, 0, j).start)
                    pl.when(has_left)(piece(c, 1, j).start)

        gated(c, act)
        if jobs[c][0] != "own" or c in by_parts:
            return
        if c == tails[0]:
            send_halo(c, 1)
        elif c == tails[1]:
            send_halo(c, 0)
            send_halo(tails[0], 0)
            send_halo(c, 1)
        else:
            send_halo(c, 0)
            send_halo(c, 1)

    for i in range(count_jobs + LAG):
        if i < count_jobs:
            mix(i)
            if i in by_parts:
                pl.when(has_right)(piece(i, 0, 0).start)
                pl.when(has_left)(piece(i, 1, 0).start)
        if i + AHEAD < count_jobs:
            start_in(i + AHEAD)
        if i >= LAG:
            settle(i - LAG)
        whiten_upto(i + AHEAD + 1)

    def wait_halos(late):
        @pl.when(has_right)
        def _():
            for c in own_jobs:
                if is_late(c, 1) == late:
                    for copy in pieces(c, 1):
                        copy.wait_recv()

        @pl.when(has_left)
        def _():
            for c in own_jobs:
                if is_late(c, 0) == late:
                    for copy in pieces(c, 0):
                        copy.wait_recv()

    load_ld.wait()
    for copy in load_windows:
        copy.wait()
    wait_halos(False)

    def early(i, carry):
        for k in range(GROUP):
            u = i * GROUP + k
            at = starts[u] - (g - 1) * blocks - SHIFT
            many = counts[u]
            parts = []
            for s in range(WIN):
                b = jnp.clip(at + s, 0, near + 1)
                if s:
                    b = b * jnp.clip(many - s, 0, 1)
                parts.append(ext_ref[b])
            sums = jnp.dot(ldv_ref[u], jnp.concatenate(parts, axis=0), preferred_element_type=jnp.float32)
            part_ref[u] = sums.astype(part_ref.dtype)
        return carry

    lax.fori_loop(0, part_ref.shape[0] // GROUP, early, 0)

    for c in order:
        def finish(c=c):
            for copy in sends_in(c) + sends_out(c):
                copy.wait_send()

        gated(c, finish)

    @pl.when(has_right)
    def _():
        first_right.wait_send()
        edge_right.wait_send()
        for c in own_jobs:
            for copy in pieces(c, 0):
                copy.wait_send()

    @pl.when(has_left)
    def _():
        first_left.wait_send()
        edge_left.wait_send()
        for c in own_jobs:
            for copy in pieces(c, 1):
                copy.wait_send()

    wait_halos(True)


def mixed_with_neighbours(z_typed, band_inverse, trait_mix, ld_untyped, win_start, win_count, groups, var_size):
    rows = z_typed.shape[0]
    blocks = rows // BLK
    jobs = job_list(blocks)
    peers = trait_mix.shape[0] // BLK
    untyped = ld_untyped.shape[0]
    work = rows + 2 * FIRST * BLK
    count = len(jobs)
    dma = pltpu.SemaphoreType.DMA
    kind = z_typed.dtype
    hbm = pl.BlockSpec(memory_space=pl.ANY)
    vmem = pl.BlockSpec(memory_space=pltpu.VMEM)
    return pl.pallas_call(
        functools.partial(mixed_kernel, jobs, blocks, groups, var_size),
        out_shape=(
            pltpu.VMEM((3 * blocks - 2 * SHIFT, BLK, BLK), kind),
            pltpu.VMEM((2 * LATE, BLK, BLK), kind),
            pltpu.VMEM(ld_untyped.shape, kind),
            pltpu.VMEM((untyped, BLK, BLK), kind),
        ),
        in_specs=[hbm] * 6,
        out_specs=(vmem, vmem, vmem, vmem),
        scratch_shapes=[
            pltpu.VMEM((rows + 2 * BLK, BLK), kind),
            pltpu.VMEM(band_inverse.shape, kind),
            pltpu.VMEM((work, BLK), kind),
            pltpu.VMEM((peers - 1, work // peers, BLK), kind),
            pltpu.VMEM(trait_mix.shape, kind),
            pltpu.VMEM((peers - 1, work // peers, BLK), kind),
            pltpu.SMEM(win_start.shape, win_start.dtype),
            pltpu.SMEM(win_count.shape, win_count.dtype),
            dma, dma, dma((2,)), dma((count,)), dma((peers, peers)),
            dma((2,)), dma((2,)),
            dma((peers - 1, count)), dma((peers - 1, count)),
            dma((peers - 1, count)), dma((peers - 1, count)),
            dma((2,)), dma((2,)),
            dma((2, peers, count)), dma((2, peers, count)),
        ],
        compiler_params=pltpu.CompilerParams(
            collective_id=0, has_side_effects=True, vmem_limit_bytes=32 * 1024 * 1024
        ),
        name="mixed_kernel",
    )(*(
        pltpu.with_memory_space_constraint(v, pltpu.HBM)
        for v in (z_typed, band_inverse, trait_mix, ld_untyped, win_start, win_count)
    ))


def impute_kernel(blocks, var_size, start_ref, count_ref, ext_ref, late_ref, ld_ref, part_ref, out_ref, fixed, sem):
    g = lax.axis_index("sec") * var_size + lax.axis_index("var")
    untyped = part_ref.shape[0]
    near = 3 * blocks - 2 * LATE

    def window(u):
        at = start_ref[u] - (g - 1) * blocks
        many = count_ref[u]
        return at, many, (at < LATE) | (at + many > LATE + near)

    def send(i, carry):
        for k in range(GROUP):
            u = i * GROUP + k
            _, _, touches = window(u)

            @pl.when(jnp.logical_not(touches))
            def _():
                pltpu.make_async_copy(part_ref.at[u], out_ref.at[u], sem).start()
        return carry

    def redo(u, carry):
        at, many, touches = window(u)

        @pl.when(touches)
        def _():
            parts = []
            for s in range(WIN):
                b = at + s
                middle = ext_ref[jnp.clip(b - SHIFT, 0, near + 1)]
                edge = late_ref[jnp.clip(jnp.where(b < LATE, b, b - near), 0, 2 * LATE - 1)]
                block = jnp.where((b < LATE) | (b >= LATE + near), edge, middle)
                parts.append(jnp.where(s < many, block, jnp.zeros_like(block)))
            sums = jnp.dot(ld_ref[u], jnp.concatenate(parts, axis=0), preferred_element_type=jnp.float32)
            fixed[u] = sums.astype(fixed.dtype)
            pltpu.make_async_copy(fixed.at[u], out_ref.at[u], sem).start()
        return carry

    lax.fori_loop(0, untyped // GROUP, send, 0)
    lax.fori_loop(0, untyped, redo, 0)
    pltpu.make_async_copy(part_ref, out_ref, sem).wait()


def impute(ext, late, ld_untyped, part, win_start, win_count, var_size):
    untyped = ld_untyped.shape[0]
    blocks = (ext.shape[0] + 2 * SHIFT) // 3
    cols = ext.shape[2]
    vmem = pl.BlockSpec(memory_space=pltpu.VMEM)
    return pl.pallas_call(
        functools.partial(impute_kernel, blocks, var_size),
        grid_spec=pltpu.PrefetchScalarGridSpec(
            num_scalar_prefetch=2,
            grid=(1,),
            in_specs=[vmem, vmem, vmem, vmem],
            out_specs=pl.BlockSpec(memory_space=pl.ANY),
            scratch_shapes=[pltpu.VMEM((untyped, BLK, cols), ext.dtype), pltpu.SemaphoreType.DMA],
        ),
        out_shape=jax.ShapeDtypeStruct((untyped, BLK, cols), ext.dtype),
        compiler_params=pltpu.CompilerParams(vmem_limit_bytes=24 * 1024 * 1024),
        name="impute_kernel",
    )(win_start, win_count, ext, late, ld_untyped, part)


def on_device(groups, var_size, z_typed, band_inverse, ld_untyped, trait_mix, win_start, win_count):
    ext, late, ld_near, part = mixed_with_neighbours(
        z_typed, band_inverse, trait_mix, ld_untyped, win_start, win_count, groups, var_size
    )
    imputed = impute(ext, late, ld_near, part, win_start, win_count, var_size)
    return imputed.reshape(ld_untyped.shape[0] * BLK, z_typed.shape[1])


def solution(mesh):
    var_size = mesh.shape["var"]
    groups = mesh.shape["sec"] * var_size
    in_specs = (
        P(("sec", "var"), "trait"),
        P(("sec", "var"), None, None),
        P(("sec", "var"), None, None),
        P(),
        P(("sec", "var")),
        P(("sec", "var")),
    )
    return jax.shard_map(
        functools.partial(on_device, groups, var_size),
        mesh=mesh, in_specs=in_specs, out_specs=P(("sec", "var"), "trait"), check_vma=False,
    )
```

time: 54.2 us -> 55.6 us (1.026)
  Pallas kernels: 54 us -> 55.4 us
    pallas_call x2, Pallas kernels: 54 us -> 55.4 us  [the longest x1 52.2 us: mixed_with_neighbours(): pl.pallas_call(functools.partial(mixed_kernel, jobs, blocks, groups, var_...]
where the time goes in v1:
time: 55.6 us; the launch traced here: 55.5 us
  Pallas kernels  55.4 us (100%)
    pallas_call x1, Pallas kernels, mixed_with_neighbours(): pl.pallas_call(functools.partial(mixed_kernel, jobs, blocks, groups, var_...  52.2 us
    pallas_call x1, Pallas kernels, impute(): pl.pallas_call(functools.partial(impute_kernel, blocks, var_size), grid_s...  3.19 us

profile of v1, /device:TPU:1, one launch (start us, length us, event | category | flops | bytes accessed | tf_op | source)
XLA Modules:
  0.0 55.5 jit_solution(11598930879740007118)
XLA Ops:
  0.0 0.0 copy-start.1
  0.0 0.0 copy-start
  0.0 52.2 %mixed_kernel.1 = (bf16[90,128,128]{2,1,0:T(8,128)(2,1)S(1)}, bf16[8,128,128]{2,1,0:T(8,128)(2,1)S(1)}, bf16[64,128,512]{2,1,0:T(8,128)(2,1)S(1)}, bf16[64,128,128]{2,1,0:T(8,128)(2,1)S(1)}) custom-call(bf16[4096,128]{1,0:T(8,128)(2,1)} %z_ref.1, bf16[32,128,384]{2,1,0:T(8,128)(2,1)} %band_ref.1, bf16[512,512]{1,0:T(8,128)(2,1)} %mix_ref.1, ...), custom_call_target="tpu_custom_call" | custom-call | tf_op jit(solution)/shard_map/mixed_kernel/pallas_call | solution.py:409
  52.2 0.0 copy-done.1
  52.2 0.0 copy-done
  52.3 3.2 %impute_kernel.1 = bf16[64,128,128]{2,1,0:T(8,128)(2,1)} custom-call(s32[64]{0:T(128)S(1)} %copy-done, s32[64]{0:T(128)S(1)} %copy-done.1, bf16[90,128,128]{2,1,0:T(8,128)(2,1)S(1)} %get-tuple-element.9.ext_ref, bf16[8,128,128]{2,1,0:T(8,128)(2,1)S(1)} %get-tuple-element.10.late_ref, bf16[64,128,512]{2,1,0:T(8,128)(2,1)S(1)} %get-tuple-element.11.ld_ref, ...), custom_call_target="tpu_custom_call" | custom-call | tf_op jit(solution)/shard_map/impute_kernel/pallas_call | solution.py:492
Async XLA Ops:
  0.0 52.2 %copy-start.1 = (s32[64]{0:T(128)S(1)}, s32[64]{0:T(128)}, u32[]{:S(2)}) copy-start(s32[64]{0:T(128)} %count_ref.3) | copy-start | bytes 772
  0.0 52.2 %copy-start = (s32[64]{0:T(128)S(1)}, s32[64]{0:T(128)}, u32[]{:S(2)}) copy-start(s32[64]{0:T(128)} %start_ref.3) | copy-start | bytes 772

commit v2 on v1

v2 whole, which is shorter than its diff:
```python
import functools

import jax
import jax.numpy as jnp
from jax import lax
from jax.experimental import pallas as pl
from jax.experimental.pallas import tpu as pltpu
from jax.sharding import PartitionSpec as P

BLK = 128
WIN = 4
FIRST = 4
LAST = 4
LATE = FIRST + LAST
CHUNK = 4
HEADS = ()
FIRST_AT = 5
AHEAD = 2
EAGER = 1
BY_PARTS = 2
GROUP = 8
REDO = 4
MESH = pl.DeviceIdType.MESH


def cut(at, stop, sizes=()):
    sizes, out = list(sizes), []
    while at < stop:
        size = min(sizes.pop(0) if sizes else CHUNK, stop - at)
        out.append((at, size))
        at += size
    return out


def job_list(blocks):
    rows = blocks * BLK
    late = blocks - LATE

    def own(kind, chunks):
        return [(kind, at, size, at * BLK, blocks + at) for at, size in chunks]

    def foreign(kind, at, size, side):
        inside = at - late
        return (kind, at, size, rows + (side * FIRST + inside) * BLK, side * LATE + inside)

    first = cut(late, late + FIRST)
    main = own("own", cut(CHUNK, late, HEADS) + cut(0, CHUNK) + cut(late + FIRST, blocks))
    taken = [foreign(kind, at, size, side) for at, size in first for side, kind in enumerate(("left", "right"))]
    return main[:FIRST_AT] + own("first", first) + main[FIRST_AT:] + taken


def mixed_kernel(
    jobs, blocks, groups, var_size,
    z_ref, band_ref, mix_ref, ld_ref, start_ref, count_ref, ext_ref, late_ref, ldv_ref, part_ref,
    zb, bandv, w, gathered, mv, results, starts, counts,
    z_sem, ld_sem, win_sem, band_sem, mix_sem, main_send, side_send, edge_recv, first_recv, in_recv, out_recv, halo_recv,
):
    t = lax.axis_index("trait")
    g = lax.axis_index("sec") * var_size + lax.axis_index("var")
    x_peer = t + 1 - 2 * lax.rem(t, 2)
    y_peer = t + 2 - 4 * (t // 2)
    far_peer = x_peer + y_peer - t
    peers = (t, x_peer, y_peer, far_peer)
    others = range(1, len(peers))
    right = {"sec": (g + 1) // var_size, "var": lax.rem(g + 1, var_size)}
    left_g = lax.rem(g + groups - 1, groups)
    left = {"sec": left_g // var_size, "var": lax.rem(left_g, var_size)}
    has_left, has_right = g > 0, g < groups - 1
    rows = blocks * BLK
    count_jobs = len(jobs)
    order = range(count_jobs)
    own_jobs = [c for c in order if jobs[c][0] == "own"]
    first_jobs = [c for c in order if jobs[c][0] == "first"]
    foreign = [c for c in order if jobs[c][0] in ("left", "right")]
    late = blocks - LATE

    barrier = pltpu.get_barrier_semaphore()

    def greet(device):
        pl.semaphore_signal(barrier, inc=1, device_id=device, device_id_type=MESH)

    def remote(src, dst, send, recv, device):
        return pltpu.make_async_remote_copy(
            src_ref=src, dst_ref=dst, send_sem=send, recv_sem=recv,
            device_id=device, device_id_type=MESH,
        )

    def gated(c, act):
        kind = jobs[c][0]
        if kind == "left":
            pl.when(has_left)(act)
        elif kind == "right":
            pl.when(has_right)(act)
        else:
            act()

    own_first = first_jobs + own_jobs

    def load_band(k):
        group = [first_jobs, own_jobs[:1], own_jobs[1:]][k]
        for c in group:
            part = pl.ds(jobs[c][1], jobs[c][2])
            pltpu.make_async_copy(band_ref.at[part], bandv.at[part], band_sem.at[k]).start()
        return sum(jobs[c][2] for c in group)

    def wait_band(k, size):
        part = pl.ds(0, size)
        pltpu.make_async_copy(band_ref.at[part], bandv.at[part], band_sem.at[k]).wait()

    def load_rows(k, at, stop):
        part = pl.ds(at * BLK, (stop - at) * BLK)
        return pltpu.make_async_copy(z_ref.at[part], zb.at[pl.ds((at + 1) * BLK, (stop - at) * BLK)], z_sem.at[k])

    cuts = [0, late - 1, late + FIRST + 1, blocks]
    load_z = [load_rows(k, *span) for k, span in enumerate(zip(cuts[:-1], cuts[1:]))]
    load_z[1].start()
    band_sizes = [load_band(0)]
    load_z[0].start()
    band_sizes.append(load_band(1))
    load_z[2].start()
    band_sizes.append(load_band(2))

    for j in others:
        greet({"trait": peers[j]})
    pl.when(has_left)(lambda: greet(left))
    pl.when(has_right)(lambda: greet(right))
    load_mix = [
        pltpu.make_async_copy(
            mix_ref.at[
                pl.ds(pl.multiple_of(taken * BLK, BLK), BLK), pl.ds(pl.multiple_of(given * BLK, BLK), BLK)
            ],
            mv.at[pl.ds(i * BLK, BLK), pl.ds(j * BLK, BLK)],
            mix_sem,
        )
        for i, taken in enumerate(peers)
        for j, given in enumerate(peers)
    ]
    load_ld = pltpu.make_async_copy(ld_ref, ldv_ref, ld_sem)
    load_windows = [
        pltpu.make_async_copy(start_ref, starts, win_sem.at[0]),
        pltpu.make_async_copy(count_ref, counts, win_sem.at[1]),
    ]

    @pl.when(jnp.logical_not(has_left))
    def _():
        zb[pl.ds(0, BLK), :] = jnp.zeros((BLK, BLK), zb.dtype)

    @pl.when(jnp.logical_not(has_right))
    def _():
        zb[pl.ds(rows + BLK, BLK), :] = jnp.zeros((BLK, BLK), zb.dtype)

    edge_right = remote(
        z_ref.at[pl.ds(rows - BLK, BLK)], zb.at[pl.ds(0, BLK)], side_send.at[0], edge_recv.at[0], right
    )
    edge_left = remote(
        z_ref.at[pl.ds(0, BLK)], zb.at[pl.ds(rows + BLK, BLK)], side_send.at[1], edge_recv.at[1], left
    )

    def whiten(c):
        _, start, size, _, _ = jobs[c]
        k = 0 if c in first_jobs else 1 if c == own_jobs[0] else 2
        if band_sizes[k]:
            wait_band(k, band_sizes[k])
            band_sizes[k] = 0
        if start + size == blocks:
            pl.when(has_right)(edge_left.wait_recv)
        if start == 0:
            pl.when(has_left)(edge_right.wait_recv)

        def one(i, carry):
            b = start + i
            row = pl.multiple_of(b * BLK, BLK)
            sums = jnp.dot(bandv[b], zb[pl.ds(row, 3 * BLK), :], preferred_element_type=jnp.float32)
            w[pl.ds(row, BLK), :] = sums.astype(w.dtype)
            return carry

        lax.fori_loop(0, size, one, 0, unroll=True)

    def first(c):
        side = 0 if jobs[c][0] == "left" else 1
        at = pl.ds(jobs[c][1] * BLK, jobs[c][2] * BLK)
        return remote(
            w.at[at], w.at[pl.ds(jobs[c][3], jobs[c][2] * BLK)],
            side_send.at[side], first_recv.at[side], (right, left)[side],
        ), (has_right, has_left)[side]

    def part_rows(c):
        return jobs[c][2] * BLK // len(peers)

    def part_of(c, peer):
        part = part_rows(c)
        return pl.ds(pl.multiple_of(jobs[c][3] + peer * part, part), part)

    def view(ref, at, c, peer):
        part = part_rows(c)
        if part == BLK:
            return ref.at[at + peer]
        row = peer * part
        return ref.at[at + row // BLK, pl.ds(pl.multiple_of(lax.rem(row, BLK), part), part)]

    def land_of(c, peer):
        return view(late_ref if c in foreign else ext_ref, jobs[c][4], c, peer)

    def share_of(c):
        return pl.ds(jobs[c][3] // len(peers), part_rows(c))

    def send_sem(c):
        return {"left": side_send.at[1], "right": side_send.at[0]}.get(jobs[c][0], main_send)

    def sends_in(c):
        return [
            remote(
                w.at[part_of(c, peers[j])], gathered.at[j - 1, share_of(c)],
                send_sem(c), in_recv.at[c], {"trait": peers[j]},
            )
            for j in others
        ]

    def sends_out(c):
        return [
            remote(
                results.at[j - 1, share_of(c)], land_of(c, t),
                send_sem(c), out_recv.at[c], {"trait": peers[j]},
            )
            for j in others
        ]

    def await_in(c):
        ref = gathered.at[:, share_of(c)]
        remote(ref, ref, send_sem(c), in_recv.at[c], {"trait": x_peer}).wait_recv()

    def await_out(c):
        ref = results.at[:, share_of(c)]
        remote(ref, ref, send_sem(c), out_recv.at[c], {"trait": x_peer}).wait_recv()

    def start_in(c):
        def act():
            if c in foreign:
                first(c)[0].wait_recv()
            for copy in sends_in(c):
                copy.start()

        gated(c, act)

    def mix(c):
        def act():
            await_in(c)
            all_traits = jnp.concatenate(
                [w[part_of(c, t), :]] + [gathered[j - 1, share_of(c), :] for j in others], axis=1
            )
            sums = jnp.dot(all_traits, mv[...], preferred_element_type=jnp.float32).astype(w.dtype)
            land_of(c, t)[...] = sums[:, :BLK]
            for j in others:
                results[j - 1, share_of(c), :] = sums[:, j * BLK : (j + 1) * BLK]
            for copy in sends_out(c):
                copy.start()

        gated(c, act)

    by_parts = own_jobs[:BY_PARTS]

    def is_late(c):
        return jobs[c][1] >= late

    def halo_at(c, side):
        start = jobs[c][1]
        if is_late(c):
            return late_ref, side * LATE + start - late
        return ext_ref, side * 2 * blocks + start

    def send_halo(c, side, part=None):
        ref, at = halo_at(c, side)
        if part is None:
            source, target = ext_ref.at[pl.ds(jobs[c][4], jobs[c][2])], ref.at[pl.ds(at, jobs[c][2])]
        else:
            source, target = view(ext_ref, jobs[c][4], c, part), view(ref, at, c, part)
        copy = remote(
            source, target, side_send.at[side], halo_recv.at[side, int(is_late(c))], right if side == 0 else left
        )
        pl.when(has_right if side == 0 else has_left)(copy.start)

    def send_halos(c, which):
        for j in which:
            for side in (0, 1):
                send_halo(c, side, None if j is None else peers[j])

    load_z[1].wait()
    pending = list(own_first)

    def whiten_upto(i):
        if i < count_jobs and i in pending:
            pending.remove(i)
            whiten(i)

    for c in first_jobs:
        whiten_upto(c)
    load_z[0].wait()
    for c in range(EAGER):
        whiten_upto(c)
    pl.semaphore_wait(barrier, len(others) + has_left.astype(jnp.int32) + has_right.astype(jnp.int32))
    for c in foreign:
        copy, sends = first(c)
        pl.when(sends)(copy.start)
    for c in range(EAGER):
        start_in(c)
    pl.when(has_right)(edge_right.start)
    pl.when(has_left)(edge_left.start)
    for copy in load_mix:
        copy.start()
    load_z[2].wait()
    for c in range(EAGER, AHEAD):
        whiten_upto(c)
    for c in range(EAGER, AHEAD):
        start_in(c)
    load_ld.start()
    for copy in load_windows:
        copy.start()
    whiten_upto(AHEAD)
    for b in (*range(late, blocks), *range(2 * blocks + late, 3 * blocks + 1)):
        ext_ref[b] = jnp.zeros((BLK, BLK), ext_ref.dtype)
    pltpu.make_async_copy(mix_ref, mv, mix_sem).wait()

    def settle(c):
        gated(c, lambda: await_out(c))
        if c in own_jobs:
            send_halos(c, others if c in by_parts else (None,))

    for i in range(count_jobs + 1):
        if i < count_jobs:
            mix(i)
            if i in by_parts:
                send_halos(i, (0,))
        if i + AHEAD < count_jobs:
            start_in(i + AHEAD)
        if i >= 1 and i - 1 not in foreign:
            settle(i - 1)
        whiten_upto(i + AHEAD + 1)

    def wait_halos(last):
        size = sum(jobs[c][2] for c in own_jobs if is_late(c) == last)
        ref = late_ref.at[pl.ds(0, size)] if last else ext_ref.at[pl.ds(0, size)]
        from_right = remote(ref, ref, side_send.at[1], halo_recv.at[1, int(last)], right)
        from_left = remote(ref, ref, side_send.at[0], halo_recv.at[0, int(last)], left)
        pl.when(has_right)(from_right.wait_recv)
        pl.when(has_left)(from_left.wait_recv)

    load_ld.wait()
    for copy in load_windows:
        copy.wait()
    wait_halos(False)

    nothing = 3 * blocks

    def early(i, carry):
        for k in range(GROUP):
            u = i * GROUP + k
            at = starts[u] - (g - 1) * blocks
            many = counts[u]
            parts = []
            for s in range(WIN):
                b = jnp.clip(at + s, 0, nothing)
                if s:
                    b = nothing + (b - nothing) * jnp.clip(many - s, 0, 1)
                parts.append(ext_ref[b])
            sums = jnp.dot(ldv_ref[u], jnp.concatenate(parts, axis=0), preferred_element_type=jnp.float32)
            part_ref[u] = sums.astype(part_ref.dtype)
        return carry

    lax.fori_loop(0, part_ref.shape[0] // GROUP, early, 0)

    for c in foreign:
        settle(c)

    def sent(size, sem):
        ref = ext_ref.at[pl.ds(0, size)]
        return remote(ref, ref, sem, edge_recv.at[0], right)

    sent(6 * blocks // len(peers), main_send).wait_send()
    side_size = blocks + 1 + 6 * FIRST // len(peers)
    pl.when(has_right)(sent(side_size, side_send.at[0]).wait_send)
    pl.when(has_left)(sent(side_size, side_send.at[1]).wait_send)
    wait_halos(True)


def mixed_with_neighbours(z_typed, band_inverse, trait_mix, ld_untyped, win_start, win_count, groups, var_size):
    rows = z_typed.shape[0]
    blocks = rows // BLK
    jobs = job_list(blocks)
    peers = trait_mix.shape[0] // BLK
    untyped = ld_untyped.shape[0]
    work = rows + 2 * FIRST * BLK
    count = len(jobs)
    dma = pltpu.SemaphoreType.DMA
    kind = z_typed.dtype
    hbm = pl.BlockSpec(memory_space=pl.ANY)
    vmem = pl.BlockSpec(memory_space=pltpu.VMEM)
    return pl.pallas_call(
        functools.partial(mixed_kernel, jobs, blocks, groups, var_size),
        out_shape=(
            pltpu.VMEM((3 * blocks + 1, BLK, BLK), kind),
            pltpu.VMEM((2 * LATE, BLK, BLK), kind),
            pltpu.VMEM(ld_untyped.shape, kind),
            pltpu.VMEM((untyped, BLK, BLK), kind),
        ),
        in_specs=[hbm] * 6,
        out_specs=(vmem, vmem, vmem, vmem),
        scratch_shapes=[
            pltpu.VMEM((rows + 2 * BLK, BLK), kind),
            pltpu.VMEM(band_inverse.shape, kind),
            pltpu.VMEM((work, BLK), kind),
            pltpu.VMEM((peers - 1, work // peers, BLK), kind),
            pltpu.VMEM(trait_mix.shape, kind),
            pltpu.VMEM((peers - 1, work // peers, BLK), kind),
            pltpu.SMEM(win_start.shape, win_start.dtype),
            pltpu.SMEM(win_count.shape, win_count.dtype),
            dma((3,)), dma, dma((2,)), dma((3,)), dma, dma, dma((2,)), dma((2,)), dma((2,)),
            dma((count,)), dma((count,)), dma((2, 2)),
        ],
        compiler_params=pltpu.CompilerParams(
            collective_id=0, has_side_effects=True, vmem_limit_bytes=32 * 1024 * 1024
        ),
        name="mixed_kernel",
    )(*(
        pltpu.with_memory_space_constraint(v, pltpu.HBM)
        for v in (z_typed, band_inverse, trait_mix, ld_untyped, win_start, win_count)
    ))


def impute_kernel(blocks, var_size, start_ref, count_ref, ext_ref, late_ref, ld_ref, part_ref, out_ref, fixed, sem):
    g = lax.axis_index("sec") * var_size + lax.axis_index("var")
    untyped = part_ref.shape[0]
    base = (g - 1) * blocks
    one, zero = jnp.int32(1), jnp.int32(0)
    spans = ((blocks - LATE, blocks), (3 * blocks - LATE, 3 * blocks))
    bounds = [zero] * 4
    for u in range(untyped):
        at = start_ref[u] - base
        for k, (low, high) in enumerate(spans):
            bounds[2 * k] += jnp.where(at + WIN <= low, one, zero)
            bounds[2 * k + 1] += jnp.where(at < high, one, zero)
    groups = untyped // REDO
    a0, a1 = bounds[0] // REDO, (bounds[1] + REDO - 1) // REDO
    b0 = jnp.maximum(a1, bounds[2] // REDO)

    def part_of(ref, i):
        return ref.at[pl.ds(i * REDO, REDO)]

    def keep(i, carry):
        pltpu.make_async_copy(part_of(part_ref, i), part_of(out_ref, i), sem).start()
        return carry

    def redo(i, carry):
        for k in range(REDO):
            u = i * REDO + k
            at = start_ref[u] - base
            many = count_ref[u]
            parts = []
            for s in range(WIN):
                b = at + s
                inside = [(b >= low) & (b < high) for low, high in spans]
                place = jnp.where(inside[0], b - spans[0][0], b - spans[1][0] + LATE)
                edge = late_ref[jnp.clip(place, 0, 2 * LATE - 1)]
                middle = ext_ref[jnp.clip(b, 0, 3 * blocks)]
                block = jnp.where(inside[0] | inside[1], edge, middle)
                parts.append(jnp.where(s < many, block, jnp.zeros_like(block)))
            sums = jnp.dot(ld_ref[u], jnp.concatenate(parts, axis=0), preferred_element_type=jnp.float32)
            fixed[u] = sums.astype(fixed.dtype)
        pltpu.make_async_copy(part_of(fixed, i), part_of(out_ref, i), sem).start()
        return carry

    lax.fori_loop(0, a0, keep, 0)
    lax.fori_loop(a1, b0, keep, 0)
    lax.fori_loop(a0, a1, redo, 0)
    lax.fori_loop(b0, groups, redo, 0)
    pltpu.make_async_copy(part_ref, out_ref, sem).wait()


def impute(ext, late, ld_untyped, part, win_start, win_count, var_size):
    untyped = ld_untyped.shape[0]
    blocks = ext.shape[0] // 3
    cols = ext.shape[2]
    vmem = pl.BlockSpec(memory_space=pltpu.VMEM)
    return pl.pallas_call(
        functools.partial(impute_kernel, blocks, var_size),
        grid_spec=pltpu.PrefetchScalarGridSpec(
            num_scalar_prefetch=2,
            grid=(1,),
            in_specs=[vmem, vmem, vmem, vmem],
            out_specs=pl.BlockSpec(memory_space=pl.ANY),
            scratch_shapes=[pltpu.VMEM((untyped, BLK, cols), ext.dtype), pltpu.SemaphoreType.DMA],
        ),
        out_shape=jax.ShapeDtypeStruct((untyped, BLK, cols), ext.dtype),
        compiler_params=pltpu.CompilerParams(vmem_limit_bytes=24 * 1024 * 1024),
        name="impute_kernel",
    )(win_start, win_count, ext, late, ld_untyped, part)


def on_device(groups, var_size, z_typed, band_inverse, ld_untyped, trait_mix, win_start, win_count):
    ext, late, ld_near, part = mixed_with_neighbours(
        z_typed, band_inverse, trait_mix, ld_untyped, win_start, win_count, groups, var_size
    )
    imputed = impute(ext, late, ld_near, part, win_start, win_count, var_size)
    return imputed.reshape(ld_untyped.shape[0] * BLK, z_typed.shape[1])


def solution(mesh):
    var_size = mesh.shape["var"]
    groups = mesh.shape["sec"] * var_size
    in_specs = (
        P(("sec", "var"), "trait"),
        P(("sec", "var"), None, None),
        P(("sec", "var"), None, None),
        P(),
        P(("sec", "var")),
        P(("sec", "var")),
    )
    return jax.shard_map(
        functools.partial(on_device, groups, var_size),
        mesh=mesh, in_specs=in_specs, out_specs=P(("sec", "var"), "trait"), check_vma=False,
    )
```

time: 55.6 us -> 46.1 us (0.83)
  Pallas kernels: 55.4 us -> 46.1 us
    pallas_call x1, Pallas kernels: 52.2 us -> 42.3 us  [mixed_with_neighbours(): pl.pallas_call(functools.partial(mixed_kernel, jobs, blocks, groups, var_...]
    pallas_call x1, Pallas kernels: 3.19 us -> 3.78 us  [impute(): pl.pallas_call(functools.partial(impute_kernel, blocks, var_size), grid_s...]
where the time goes in v2:
time: 46.1 us
  Pallas kernels  46.1 us (100%)
    pallas_call x1, Pallas kernels, mixed_with_neighbours(): pl.pallas_call(functools.partial(mixed_kernel, jobs, blocks, groups, var_...  42.3 us
    pallas_call x1, Pallas kernels, impute(): pl.pallas_call(functools.partial(impute_kernel, blocks, var_size), grid_s...  3.78 us

profile of v2, /device:TPU:1, one launch (start us, length us, event | category | flops | bytes accessed | tf_op | source)
XLA Modules:
  0.0 46.1 jit_solution(291721485230278024)
XLA Ops:
  0.0 0.0 copy-start.1
  0.0 0.0 copy-start
  0.0 42.3 %mixed_kernel.1 = (bf16[97,128,128]{2,1,0:T(8,128)(2,1)S(1)}, bf16[16,128,128]{2,1,0:T(8,128)(2,1)S(1)}, bf16[64,128,512]{2,1,0:T(8,128)(2,1)S(1)}, bf16[64,128,128]{2,1,0:T(8,128)(2,1)S(1)}) custom-call(bf16[4096,128]{1,0:T(8,128)(2,1)} %z_ref.1, bf16[32,128,384]{2,1,0:T(8,128)(2,1)} %band_ref.1, bf16[512,512]{1,0:T(8,128)(2,1)} %mix_ref.1, ...), custom_call_target="tpu_custom_call" | custom-call | tf_op jit(solution)/shard_map/mixed_kernel/pallas_call | solution.py:397
  42.3 0.0 copy-done.1
  42.3 0.0 copy-done
  42.3 3.8 %impute_kernel.1 = bf16[64,128,128]{2,1,0:T(8,128)(2,1)} custom-call(s32[64]{0:T(128)S(1)} %copy-done, s32[64]{0:T(128)S(1)} %copy-done.1, bf16[97,128,128]{2,1,0:T(8,128)(2,1)S(1)} %get-tuple-element.9.ext_ref, bf16[16,128,128]{2,1,0:T(8,128)(2,1)S(1)} %get-tuple-element.10.late_ref, bf16[64,128,512]{2,1,0:T(8,128)(2,1)S(1)} %get-tuple-element.11.ld_ref, ...), custom_call_target="tpu_custom_call" | custom-call | tf_op jit(solution)/shard_map/impute_kernel/pallas_call | solution.py:483
Async XLA Ops:
  0.0 42.3 %copy-start.1 = (s32[64]{0:T(128)S(1)}, s32[64]{0:T(128)}, u32[]{:S(2)}) copy-start(s32[64]{0:T(128)} %count_ref.3) | copy-start | bytes 772
  0.0 42.3 %copy-start = (s32[64]{0:T(128)S(1)}, s32[64]{0:T(128)}, u32[]{:S(2)}) copy-start(s32[64]{0:T(128)} %start_ref.3) | copy-start | bytes 772

commit v3 on v2

--- a/solution.py
+++ b/solution.py
@@ -10,16 +10,16 @@
 BLK = 128
 WIN = 4
 FIRST = 4
-LAST = 4
-LATE = FIRST + LAST
+LAST = 8
 CHUNK = 4
 HEADS = ()
 FIRST_AT = 5
 AHEAD = 2
 EAGER = 1
-BY_PARTS = 2
+BY_PARTS = 4
 GROUP = 8
 REDO = 4
+DELAY = 1
 MESH = pl.DeviceIdType.MESH
 
 
@@ -34,17 +34,17 @@
 
 def job_list(blocks):
     rows = blocks * BLK
-    late = blocks - LATE
+    late = blocks - LAST
+    begin = late - FIRST
 
     def own(kind, chunks):
         return [(kind, at, size, at * BLK, blocks + at) for at, size in chunks]
 
     def foreign(kind, at, size, side):
-        inside = at - late
-        return (kind, at, size, rows + (side * FIRST + inside) * BLK, side * LATE + inside)
-
-    first = cut(late, late + FIRST)
-    main = own("own", cut(CHUNK, late, HEADS) + cut(0, CHUNK) + cut(late + FIRST, blocks))
+        return (kind, at, size, rows + (side * FIRST + at - begin) * BLK, side * 2 * blocks + at)
+
+    first = cut(begin, late)
+    main = own("own", cut(CHUNK, begin, HEADS) + cut(0, CHUNK) + cut(late, blocks))
     taken = [foreign(kind, at, size, side) for at, size in first for side, kind in enumerate(("left", "right"))]
     return main[:FIRST_AT] + own("first", first) + main[FIRST_AT:] + taken
 
@@ -72,7 +72,8 @@
     own_jobs = [c for c in order if jobs[c][0] == "own"]
     first_jobs = [c for c in order if jobs[c][0] == "first"]
     foreign = [c for c in order if jobs[c][0] in ("left", "right")]
-    late = blocks - LATE
+    late = blocks - LAST
+    begin = late - FIRST
 
     barrier = pltpu.get_barrier_semaphore()
 
@@ -111,14 +112,12 @@
         part = pl.ds(at * BLK, (stop - at) * BLK)
         return pltpu.make_async_copy(z_ref.at[part], zb.at[pl.ds((at + 1) * BLK, (stop - at) * BLK)], z_sem.at[k])
 
-    cuts = [0, late - 1, late + FIRST + 1, blocks]
+    cuts = [0, CHUNK - 1, 2 * CHUNK + 1, begin - 1, late + 1, blocks]
     load_z = [load_rows(k, *span) for k, span in enumerate(zip(cuts[:-1], cuts[1:]))]
+    load_z[3].start()
+    band_sizes = [load_band(0)]
     load_z[1].start()
-    band_sizes = [load_band(0)]
-    load_z[0].start()
     band_sizes.append(load_band(1))
-    load_z[2].start()
-    band_sizes.append(load_band(2))
 
     for j in others:
         greet({"trait": peers[j]})
@@ -181,7 +180,7 @@
         at = pl.ds(jobs[c][1] * BLK, jobs[c][2] * BLK)
         return remote(
             w.at[at], w.at[pl.ds(jobs[c][3], jobs[c][2] * BLK)],
-            side_send.at[side], first_recv.at[side], (right, left)[side],
+            side_send.at[side], first_recv.at[foreign.index(c)], (right, left)[side],
         ), (has_right, has_left)[side]
 
     def part_rows(c):
@@ -199,7 +198,7 @@
         return ref.at[at + row // BLK, pl.ds(pl.multiple_of(lax.rem(row, BLK), part), part)]
 
     def land_of(c, peer):
-        return view(late_ref if c in foreign else ext_ref, jobs[c][4], c, peer)
+        return view(ext_ref, jobs[c][4], c, peer)
 
     def share_of(c):
         return pl.ds(jobs[c][3] // len(peers), part_rows(c))
@@ -265,10 +264,10 @@
     def halo_at(c, side):
         start = jobs[c][1]
         if is_late(c):
-            return late_ref, side * LATE + start - late
+            return late_ref, side * LAST + start - late
         return ext_ref, side * 2 * blocks + start
 
-    def send_halo(c, side, part=None):
+    def send_halo(c, side, part):
         ref, at = halo_at(c, side)
         if part is None:
             source, target = ext_ref.at[pl.ds(jobs[c][4], jobs[c][2])], ref.at[pl.ds(at, jobs[c][2])]
@@ -277,14 +276,29 @@
         copy = remote(
             source, target, side_send.at[side], halo_recv.at[side, int(is_late(c))], right if side == 0 else left
         )
-        pl.when(has_right if side == 0 else has_left)(copy.start)
+        return copy
+
+    at_end = has_left & (g == var_size - 1)
+    held = []
 
     def send_halos(c, which):
-        for j in which:
-            for side in (0, 1):
-                send_halo(c, side, None if j is None else peers[j])
-
-    load_z[1].wait()
+        parts = [None if j is None else peers[j] for j in which]
+        for part in parts:
+            pl.when(has_right)(send_halo(c, 0, part).start)
+            pl.when(has_left & jnp.logical_not(at_end))(send_halo(c, 1, part).start)
+        held.append([send_halo(c, 1, part) for part in parts])
+        release(DELAY)
+
+    def release(keep):
+        while len(held) > keep:
+            copies = held.pop(0)
+
+            @pl.when(at_end)
+            def _():
+                for copy in copies:
+                    copy.start()
+
+    load_z[3].wait()
     pending = list(own_first)
 
     def whiten_upto(i):
@@ -294,7 +308,10 @@
 
     for c in first_jobs:
         whiten_upto(c)
-    load_z[0].wait()
+    for k in (2, 0, 4):
+        load_z[k].start()
+    band_sizes.append(load_band(2))
+    load_z[1].wait()
     for c in range(EAGER):
         whiten_upto(c)
     pl.semaphore_wait(barrier, len(others) + has_left.astype(jnp.int32) + has_right.astype(jnp.int32))
@@ -307,7 +324,8 @@
     pl.when(has_left)(edge_left.start)
     for copy in load_mix:
         copy.start()
-    load_z[2].wait()
+    for k in (2, 0, 4):
+        load_z[k].wait()
     for c in range(EAGER, AHEAD):
         whiten_upto(c)
     for c in range(EAGER, AHEAD):
@@ -336,6 +354,8 @@
             settle(i - 1)
         whiten_upto(i + AHEAD + 1)
 
+    release(0)
+
     def wait_halos(last):
         size = sum(jobs[c][2] for c in own_jobs if is_late(c) == last)
         ref = late_ref.at[pl.ds(0, size)] if last else ext_ref.at[pl.ds(0, size)]
@@ -344,6 +364,8 @@
         pl.when(has_right)(from_right.wait_recv)
         pl.when(has_left)(from_left.wait_recv)
 
+    for c in foreign:
+        settle(c)
     load_ld.wait()
     for copy in load_windows:
         copy.wait()
@@ -368,9 +390,6 @@
 
     lax.fori_loop(0, part_ref.shape[0] // GROUP, early, 0)
 
-    for c in foreign:
-        settle(c)
-
     def sent(size, sem):
         ref = ext_ref.at[pl.ds(0, size)]
         return remote(ref, ref, sem, edge_recv.at[0], right)
@@ -390,6 +409,7 @@
     untyped = ld_untyped.shape[0]
     work = rows + 2 * FIRST * BLK
     count = len(jobs)
+    taken = sum(job[0] in ("left", "right") for job in jobs)
     dma = pltpu.SemaphoreType.DMA
     kind = z_typed.dtype
     hbm = pl.BlockSpec(memory_space=pl.ANY)
@@ -398,7 +418,7 @@
         functools.partial(mixed_kernel, jobs, blocks, groups, var_size),
         out_shape=(
             pltpu.VMEM((3 * blocks + 1, BLK, BLK), kind),
-            pltpu.VMEM((2 * LATE, BLK, BLK), kind),
+            pltpu.VMEM((2 * LAST, BLK, BLK), kind),
             pltpu.VMEM(ld_untyped.shape, kind),
             pltpu.VMEM((untyped, BLK, BLK), kind),
         ),
@@ -413,7 +433,7 @@
             pltpu.VMEM((peers - 1, work // peers, BLK), kind),
             pltpu.SMEM(win_start.shape, win_start.dtype),
             pltpu.SMEM(win_count.shape, win_count.dtype),
-            dma((3,)), dma, dma((2,)), dma((3,)), dma, dma, dma((2,)), dma((2,)), dma((2,)),
+            dma((5,)), dma, dma((2,)), dma((3,)), dma, dma, dma((2,)), dma((2,)), dma((taken,)),
             dma((count,)), dma((count,)), dma((2, 2)),
         ],
         compiler_params=pltpu.CompilerParams(
@@ -431,7 +451,7 @@
     untyped = part_ref.shape[0]
     base = (g - 1) * blocks
     one, zero = jnp.int32(1), jnp.int32(0)
-    spans = ((blocks - LATE, blocks), (3 * blocks - LATE, 3 * blocks))
+    spans = ((blocks - LAST, blocks), (3 * blocks - LAST, 3 * blocks))
     bounds = [zero] * 4
     for u in range(untyped):
         at = start_ref[u] - base
@@ -458,8 +478,8 @@
             for s in range(WIN):
                 b = at + s
                 inside = [(b >= low) & (b < high) for low, high in spans]
-                place = jnp.where(inside[0], b - spans[0][0], b - spans[1][0] + LATE)
-                edge = late_ref[jnp.clip(place, 0, 2 * LATE - 1)]
+                place = jnp.where(inside[0], b - spans[0][0], b - spans[1][0] + LAST)
+                edge = late_ref[jnp.clip(place, 0, 2 * LAST - 1)]
                 middle = ext_ref[jnp.clip(b, 0, 3 * blocks)]
                 block = jnp.where(inside[0] | inside[1], edge, middle)
                 parts.append(jnp.where(s < many, block, jnp.zeros_like(block)))

time: 46.1 us -> 44 us (0.954)
  Pallas kernels: 46.1 us -> 43.7 us
    pallas_call x1, Pallas kernels: 42.3 us -> 40.3 us  [mixed_with_neighbours(): pl.pallas_call(functools.partial(mixed_kernel, jobs, blocks, groups, var_...]
where the time goes in v3:
time: 44 us; the launch traced here: 43.7 us
  Pallas kernels  43.7 us (99%)
    pallas_call x1, Pallas kernels, mixed_with_neighbours(): pl.pallas_call(functools.partial(mixed_kernel, jobs, blocks, groups, var_...  40.3 us
    pallas_call x1, Pallas kernels, impute(): pl.pallas_call(functools.partial(impute_kernel, blocks, var_size), grid_s...  3.41 us

profile of v3, /device:TPU:1, one launch (start us, length us, event | category | flops | bytes accessed | tf_op | source)
XLA Modules:
  0.0 43.7 jit_solution(6888233484508261643)
XLA Ops:
  0.0 0.0 copy-start.1
  0.0 0.0 copy-start
  0.0 40.3 %mixed_kernel.1 = (bf16[97,128,128]{2,1,0:T(8,128)(2,1)S(1)}, bf16[16,128,128]{2,1,0:T(8,128)(2,1)S(1)}, bf16[64,128,512]{2,1,0:T(8,128)(2,1)S(1)}, bf16[64,128,128]{2,1,0:T(8,128)(2,1)S(1)}) custom-call(bf16[4096,128]{1,0:T(8,128)(2,1)} %z_ref.1, bf16[32,128,384]{2,1,0:T(8,128)(2,1)} %band_ref.1, bf16[512,512]{1,0:T(8,128)(2,1)} %mix_ref.1, ...), custom_call_target="tpu_custom_call" | custom-call | tf_op jit(solution)/shard_map/mixed_kernel/pallas_call | solution.py:417
  40.3 0.0 copy-done.1
  40.3 0.0 copy-done
  40.3 3.4 %impute_kernel.1 = bf16[64,128,128]{2,1,0:T(8,128)(2,1)} custom-call(s32[64]{0:T(128)S(1)} %copy-done, s32[64]{0:T(128)S(1)} %copy-done.1, bf16[97,128,128]{2,1,0:T(8,128)(2,1)S(1)} %get-tuple-element.9.ext_ref, bf16[16,128,128]{2,1,0:T(8,128)(2,1)S(1)} %get-tuple-element.10.late_ref, bf16[64,128,512]{2,1,0:T(8,128)(2,1)S(1)} %get-tuple-element.11.ld_ref, ...), custom_call_target="tpu_custom_call" | custom-call | tf_op jit(solution)/shard_map/impute_kernel/pallas_call | solution.py:503
Async XLA Ops:
  0.0 40.3 %copy-start.1 = (s32[64]{0:T(128)S(1)}, s32[64]{0:T(128)}, u32[]{:S(2)}) copy-start(s32[64]{0:T(128)} %count_ref.3) | copy-start | bytes 772
  0.0 40.3 %copy-start = (s32[64]{0:T(128)S(1)}, s32[64]{0:T(128)}, u32[]{:S(2)}) copy-start(s32[64]{0:T(128)} %start_ref.3) | copy-start | bytes 772

commit v4 on v3

--- a/solution.py
+++ b/solution.py
@@ -11,6 +11,8 @@
 WIN = 4
 FIRST = 4
 LAST = 8
+FOREIGN_LATE = 0
+LATE = LAST + FOREIGN_LATE * FIRST
 CHUNK = 4
 HEADS = ()
 FIRST_AT = 5
@@ -18,7 +20,7 @@
 EAGER = 1
 BY_PARTS = 4
 GROUP = 8
-REDO = 4
+REDO = 8
 DELAY = 1
 MESH = pl.DeviceIdType.MESH
 
@@ -41,7 +43,8 @@
         return [(kind, at, size, at * BLK, blocks + at) for at, size in chunks]
 
     def foreign(kind, at, size, side):
-        return (kind, at, size, rows + (side * FIRST + at - begin) * BLK, side * 2 * blocks + at)
+        land = side * LATE + at - (blocks - LATE) if FOREIGN_LATE else side * 2 * blocks + at
+        return (kind, at, size, rows + (side * FIRST + at - begin) * BLK, land)
 
     first = cut(begin, late)
     main = own("own", cut(CHUNK, begin, HEADS) + cut(0, CHUNK) + cut(late, blocks))
@@ -51,8 +54,8 @@
 
 def mixed_kernel(
     jobs, blocks, groups, var_size,
-    z_ref, band_ref, mix_ref, ld_ref, start_ref, count_ref, ext_ref, late_ref, ldv_ref, part_ref,
-    zb, bandv, w, gathered, mv, results, starts, counts,
+    z_ref, band_ref, mix_ref, ld_ref, start_ref, count_ref, ext_ref, ldv_ref, part_ref, starts, counts, touched,
+    zb, bandv, w, gathered, mv, results, late_ref,
     z_sem, ld_sem, win_sem, band_sem, mix_sem, main_send, side_send, edge_recv, first_recv, in_recv, out_recv, halo_recv,
 ):
     t = lax.axis_index("trait")
@@ -80,6 +83,11 @@
     def greet(device):
         pl.semaphore_signal(barrier, inc=1, device_id=device, device_id_type=MESH)
 
+    for j in others:
+        greet({"trait": peers[j]})
+    pl.when(has_left)(lambda: greet(left))
+    pl.when(has_right)(lambda: greet(right))
+
     def remote(src, dst, send, recv, device):
         return pltpu.make_async_remote_copy(
             src_ref=src, dst_ref=dst, send_sem=send, recv_sem=recv,
@@ -119,10 +127,6 @@
     load_z[1].start()
     band_sizes.append(load_band(1))
 
-    for j in others:
-        greet({"trait": peers[j]})
-    pl.when(has_left)(lambda: greet(left))
-    pl.when(has_right)(lambda: greet(right))
     load_mix = [
         pltpu.make_async_copy(
             mix_ref.at[
@@ -198,7 +202,7 @@
         return ref.at[at + row // BLK, pl.ds(pl.multiple_of(lax.rem(row, BLK), part), part)]
 
     def land_of(c, peer):
-        return view(ext_ref, jobs[c][4], c, peer)
+        return view(late_ref if FOREIGN_LATE and c in foreign else ext_ref, jobs[c][4], c, peer)
 
     def share_of(c):
         return pl.ds(jobs[c][3] // len(peers), part_rows(c))
@@ -264,7 +268,7 @@
     def halo_at(c, side):
         start = jobs[c][1]
         if is_late(c):
-            return late_ref, side * LAST + start - late
+            return late_ref, side * LATE + start - (blocks - LATE)
         return ext_ref, side * 2 * blocks + start
 
     def send_halo(c, side, part):
@@ -334,9 +338,20 @@
     for copy in load_windows:
         copy.start()
     whiten_upto(AHEAD)
-    for b in (*range(late, blocks), *range(2 * blocks + late, 3 * blocks + 1)):
+    for b in (*range(blocks - LATE, blocks), *range(3 * blocks - LATE, 3 * blocks + 1)):
         ext_ref[b] = jnp.zeros((BLK, BLK), ext_ref.dtype)
     pltpu.make_async_copy(mix_ref, mv, mix_sem).wait()
+    for copy in load_windows:
+        copy.wait()
+    for i in range(part_ref.shape[0] // REDO):
+        found = 0
+        for u in range(i * REDO, (i + 1) * REDO):
+            at = starts[u] - (g - 1) * blocks
+            stop = at + counts[u]
+            in_left = jnp.clip(blocks - at, 0, 1) * jnp.clip(stop - (blocks - LATE), 0, 1)
+            in_right = jnp.clip(stop - (3 * blocks - LATE), 0, 1)
+            found = found + in_left + in_right
+        touched[i] = found
 
     def settle(c):
         gated(c, lambda: await_out(c))
@@ -364,11 +379,10 @@
         pl.when(has_right)(from_right.wait_recv)
         pl.when(has_left)(from_left.wait_recv)
 
-    for c in foreign:
-        settle(c)
+    if not FOREIGN_LATE:
+        for c in foreign:
+            settle(c)
     load_ld.wait()
-    for copy in load_windows:
-        copy.wait()
     wait_halos(False)
 
     nothing = 3 * blocks
@@ -390,6 +404,10 @@
 
     lax.fori_loop(0, part_ref.shape[0] // GROUP, early, 0)
 
+    if FOREIGN_LATE:
+        for c in foreign:
+            settle(c)
+
     def sent(size, sem):
         ref = ext_ref.at[pl.ds(0, size)]
         return remote(ref, ref, sem, edge_recv.at[0], right)
@@ -399,6 +417,9 @@
     pl.when(has_right)(sent(side_size, side_send.at[0]).wait_send)
     pl.when(has_left)(sent(side_size, side_send.at[1]).wait_send)
     wait_halos(True)
+    for side in (0, 1):
+        for k in range(LATE):
+            ext_ref[(2 * side + 1) * blocks - LATE + k] = late_ref[side * LATE + k]
 
 
 def mixed_with_neighbours(z_typed, band_inverse, trait_mix, ld_untyped, win_start, win_count, groups, var_size):
@@ -414,16 +435,19 @@
     kind = z_typed.dtype
     hbm = pl.BlockSpec(memory_space=pl.ANY)
     vmem = pl.BlockSpec(memory_space=pltpu.VMEM)
+    smem = pl.BlockSpec(memory_space=pltpu.SMEM)
     return pl.pallas_call(
         functools.partial(mixed_kernel, jobs, blocks, groups, var_size),
         out_shape=(
             pltpu.VMEM((3 * blocks + 1, BLK, BLK), kind),
-            pltpu.VMEM((2 * LAST, BLK, BLK), kind),
             pltpu.VMEM(ld_untyped.shape, kind),
             pltpu.VMEM((untyped, BLK, BLK), kind),
+            pltpu.SMEM(win_start.shape, win_start.dtype),
+            pltpu.SMEM(win_count.shape, win_count.dtype),
+            pltpu.SMEM((untyped // REDO,), win_count.dtype),
         ),
         in_specs=[hbm] * 6,
-        out_specs=(vmem, vmem, vmem, vmem),
+        out_specs=(vmem, vmem, vmem, smem, smem, smem),
         scratch_shapes=[
             pltpu.VMEM((rows + 2 * BLK, BLK), kind),
             pltpu.VMEM(band_inverse.shape, kind),
@@ -431,8 +455,7 @@
             pltpu.VMEM((peers - 1, work // peers, BLK), kind),
             pltpu.VMEM(trait_mix.shape, kind),
             pltpu.VMEM((peers - 1, work // peers, BLK), kind),
-            pltpu.SMEM(win_start.shape, win_start.dtype),
-            pltpu.SMEM(win_count.shape, win_count.dtype),
+            pltpu.VMEM((2 * LATE, BLK, BLK), kind),
             dma((5,)), dma, dma((2,)), dma((3,)), dma, dma, dma((2,)), dma((2,)), dma((taken,)),
             dma((count,)), dma((count,)), dma((2, 2)),
         ],
@@ -446,80 +469,55 @@
     ))
 
 
-def impute_kernel(blocks, var_size, start_ref, count_ref, ext_ref, late_ref, ld_ref, part_ref, out_ref, fixed, sem):
+def impute_kernel(blocks, var_size, start_ref, count_ref, touched, ext_ref, ld_ref, part_ref, out_ref, fixed, sem):
     g = lax.axis_index("sec") * var_size + lax.axis_index("var")
-    untyped = part_ref.shape[0]
-    base = (g - 1) * blocks
-    one, zero = jnp.int32(1), jnp.int32(0)
-    spans = ((blocks - LAST, blocks), (3 * blocks - LAST, 3 * blocks))
-    bounds = [zero] * 4
-    for u in range(untyped):
-        at = start_ref[u] - base
-        for k, (low, high) in enumerate(spans):
-            bounds[2 * k] += jnp.where(at + WIN <= low, one, zero)
-            bounds[2 * k + 1] += jnp.where(at < high, one, zero)
-    groups = untyped // REDO
-    a0, a1 = bounds[0] // REDO, (bounds[1] + REDO - 1) // REDO
-    b0 = jnp.maximum(a1, bounds[2] // REDO)
-
-    def part_of(ref, i):
-        return ref.at[pl.ds(i * REDO, REDO)]
-
-    def keep(i, carry):
-        pltpu.make_async_copy(part_of(part_ref, i), part_of(out_ref, i), sem).start()
-        return carry
-
-    def redo(i, carry):
-        for k in range(REDO):
-            u = i * REDO + k
-            at = start_ref[u] - base
+    nothing = 3 * blocks
+
+    def send(ref, i):
+        part = pl.ds(i * REDO, REDO)
+        pltpu.make_async_copy(ref.at[part], out_ref.at[part], sem).start()
+
+    def redo(i):
+        for u in range(i * REDO, (i + 1) * REDO):
+            at = start_ref[u] - (g - 1) * blocks
             many = count_ref[u]
             parts = []
             for s in range(WIN):
-                b = at + s
-                inside = [(b >= low) & (b < high) for low, high in spans]
-                place = jnp.where(inside[0], b - spans[0][0], b - spans[1][0] + LAST)
-                edge = late_ref[jnp.clip(place, 0, 2 * LAST - 1)]
-                middle = ext_ref[jnp.clip(b, 0, 3 * blocks)]
-                block = jnp.where(inside[0] | inside[1], edge, middle)
-                parts.append(jnp.where(s < many, block, jnp.zeros_like(block)))
+                b = jnp.clip(at + s, 0, nothing)
+                parts.append(ext_ref[jnp.where(s < many, b, nothing) if s else b])
             sums = jnp.dot(ld_ref[u], jnp.concatenate(parts, axis=0), preferred_element_type=jnp.float32)
             fixed[u] = sums.astype(fixed.dtype)
-        pltpu.make_async_copy(part_of(fixed, i), part_of(out_ref, i), sem).start()
-        return carry
-
-    lax.fori_loop(0, a0, keep, 0)
-    lax.fori_loop(a1, b0, keep, 0)
-    lax.fori_loop(a0, a1, redo, 0)
-    lax.fori_loop(b0, groups, redo, 0)
+        send(fixed, i)
+
+    for i in range(part_ref.shape[0] // REDO):
+        pl.when(touched[i] == 0)(functools.partial(send, part_ref, i))
+    for i in range(part_ref.shape[0] // REDO):
+        pl.when(touched[i] != 0)(functools.partial(redo, i))
     pltpu.make_async_copy(part_ref, out_ref, sem).wait()
 
 
-def impute(ext, late, ld_untyped, part, win_start, win_count, var_size):
+def impute(ext, ld_untyped, part, starts, counts, touched, var_size):
     untyped = ld_untyped.shape[0]
     blocks = ext.shape[0] // 3
     cols = ext.shape[2]
     vmem = pl.BlockSpec(memory_space=pltpu.VMEM)
+    smem = pl.BlockSpec(memory_space=pltpu.SMEM)
     return pl.pallas_call(
         functools.partial(impute_kernel, blocks, var_size),
-        grid_spec=pltpu.PrefetchScalarGridSpec(
-            num_scalar_prefetch=2,
-            grid=(1,),
-            in_specs=[vmem, vmem, vmem, vmem],
-            out_specs=pl.BlockSpec(memory_space=pl.ANY),
-            scratch_shapes=[pltpu.VMEM((untyped, BLK, cols), ext.dtype), pltpu.SemaphoreType.DMA],
-        ),
+        in_specs=[smem, smem, smem, vmem, vmem, vmem],
+        out_specs=pl.BlockSpec(memory_space=pl.ANY),
+        scratch_shapes=[pltpu.VMEM((untyped, BLK, cols), ext.dtype), pltpu.SemaphoreType.DMA],
         out_shape=jax.ShapeDtypeStruct((untyped, BLK, cols), ext.dtype),
         compiler_params=pltpu.CompilerParams(vmem_limit_bytes=24 * 1024 * 1024),
         name="impute_kernel",
-    )(win_start, win_count, ext, late, ld_untyped, part)
+    )(starts, counts, touched, ext, ld_untyped, part)
 
 
 def on_device(groups, var_size, z_typed, band_inverse, ld_untyped, trait_mix, win_start, win_count):
-    ext, late, ld_near, part = mixed_with_neighbours(
+    ext, ld_near, part, starts, counts, touched = mixed_with_neighbours(
         z_typed, band_inverse, trait_mix, ld_untyped, win_start, win_count, groups, var_size
     )
-    imputed = impute(ext, late, ld_near, part, win_start, win_count, var_size)
+    imputed = impute(ext, ld_near, part, starts, counts, touched, var_size)
     return imputed.reshape(ld_untyped.shape[0] * BLK, z_typed.shape[1])
 
 

time: 44 us -> 43.2 us (0.982); the launches traced: 43.7 us -> 42.4 us
  Pallas kernels: 43.7 us -> 42.4 us
    pallas_call x1, Pallas kernels: 3.41 us -> 2.09 us  [impute(): pl.pallas_call(functools.partial(impute_kernel, blocks, var_size), in_spe...]
where the time goes in v4:
time: 43.2 us; the launch traced here: 42.4 us
  Pallas kernels  42.4 us (98%)
    pallas_call x1, Pallas kernels, mixed_with_neighbours(): pl.pallas_call(functools.partial(mixed_kernel, jobs, blocks, groups, var_...  40.3 us
    pallas_call x1, Pallas kernels, impute(): pl.pallas_call(functools.partial(impute_kernel, blocks, var_size), in_spe...  2.09 us

profile of v4, /device:TPU:1, one launch (start us, length us, event | category | flops | bytes accessed | tf_op | source)
XLA Modules:
  0.0 42.4 jit_solution(1555947388982338630)
XLA Ops:
  0.0 40.3 %mixed_kernel.1 = (bf16[97,128,128]{2,1,0:T(8,128)(2,1)S(1)}, bf16[64,128,512]{2,1,0:T(8,128)(2,1)S(1)}, bf16[64,128,128]{2,1,0:T(8,128)(2,1)S(1)}, s32[64]{0:T(128)S(4)}, s32[64]{0:T(128)S(4)}, /*index=5*/s32[8]{0:T(128)S(4)}) custom-call(bf16[4096,128]{1,0:T(8,128)(2,1)} %z_ref.1, bf16[32,128,384]{2,1,0:T(8,128)(2,1)} %band_ref.1, ...), custom_call_target="tpu_custom_call" | custom-call | tf_op jit(solution)/shard_map/mixed_kernel/pallas_call | solution.py:439
  40.4 2.1 %impute_kernel.1 = bf16[64,128,128]{2,1,0:T(8,128)(2,1)} custom-call(s32[64]{0:T(128)S(4)} %get-tuple-element.11.start_ref, s32[64]{0:T(128)S(4)} %get-tuple-element.12.count_ref, s32[8]{0:T(128)S(4)} %get-tuple-element.13.touched, bf16[97,128,128]{2,1,0:T(8,128)(2,1)S(1)} %get-tuple-element.14.ext_ref, bf16[64,128,512]{2,1,0:T(8,128)(2,1)S(1)} %get-tuple-element.15.ld_ref, ...), custom_call_target="tpu_custom_call" | custom-call | tf_op jit(solution)/shard_map/impute_kernel/pallas_call | solution.py:505

commit v5 on v4

--- a/solution.py
+++ b/solution.py
@@ -11,14 +11,15 @@
 WIN = 4
 FIRST = 4
 LAST = 8
-FOREIGN_LATE = 0
+FOREIGN_LATE = 1
 LATE = LAST + FOREIGN_LATE * FIRST
 CHUNK = 4
 HEADS = ()
 FIRST_AT = 5
 AHEAD = 2
 EAGER = 1
-BY_PARTS = 4
+BY_PARTS = 3
+SPLIT = 3
 GROUP = 8
 REDO = 8
 DELAY = 1
@@ -223,10 +224,17 @@
         return [
             remote(
                 results.at[j - 1, share_of(c)], land_of(c, t),
-                send_sem(c), out_recv.at[c], {"trait": peers[j]},
+                send_sem(c), out_sem(c, j), {"trait": peers[j]},
             )
             for j in others
         ]
+
+    def out_sem(c, j):
+        return out_recv.at[count_jobs + 2 * c + j - 2 if c in own_jobs[:SPLIT] and j > 1 else c]
+
+    def await_part(c, j):
+        ref = results.at[j - 1, share_of(c)]
+        remote(ref, ref, send_sem(c), out_sem(c, j), {"trait": x_peer}).wait_recv()
 
     def await_in(c):
         ref = gathered.at[:, share_of(c)]
@@ -290,12 +298,15 @@
         for part in parts:
             pl.when(has_right)(send_halo(c, 0, part).start)
             pl.when(has_left & jnp.logical_not(at_end))(send_halo(c, 1, part).start)
-        held.append([send_halo(c, 1, part) for part in parts])
+        if held and held[-1][0] == c:
+            held[-1][1].extend(send_halo(c, 1, part) for part in parts)
+        else:
+            held.append((c, [send_halo(c, 1, part) for part in parts]))
         release(DELAY)
 
     def release(keep):
         while len(held) > keep:
-            copies = held.pop(0)
+            copies = held.pop(0)[1]
 
             @pl.when(at_end)
             def _():
@@ -354,6 +365,11 @@
         touched[i] = found
 
     def settle(c):
+        if c in own_jobs[:SPLIT]:
+            for j in others:
+                await_part(c, j)
+                send_halos(c, (j,))
+            return
         gated(c, lambda: await_out(c))
         if c in own_jobs:
             send_halos(c, others if c in by_parts else (None,))
@@ -457,7 +473,7 @@
             pltpu.VMEM((peers - 1, work // peers, BLK), kind),
             pltpu.VMEM((2 * LATE, BLK, BLK), kind),
             dma((5,)), dma, dma((2,)), dma((3,)), dma, dma, dma((2,)), dma((2,)), dma((taken,)),
-            dma((count,)), dma((count,)), dma((2, 2)),
+            dma((count,)), dma((count + 2 * SPLIT,)), dma((2, 2)),
         ],
         compiler_params=pltpu.CompilerParams(
             collective_id=0, has_side_effects=True, vmem_limit_bytes=32 * 1024 * 1024

time: 43.2 us -> 42.9 us (level)
  the two profiles are of different devices: /device:TPU:1 before, /device:TPU:0 now
where the time goes in v5:
time: 42.9 us; the launch traced here: 42.6 us
  Pallas kernels  42.6 us (99%)
    pallas_call x1, Pallas kernels, mixed_with_neighbours(): pl.pallas_call(functools.partial(mixed_kernel, jobs, blocks, groups, var_...  41.3 us
    pallas_call x1, Pallas kernels, impute(): pl.pallas_call(functools.partial(impute_kernel, blocks, var_size), in_spe...  1.33 us

profile of v5, /device:TPU:0, one launch (start us, length us, event | category | flops | bytes accessed | tf_op | source)
XLA Modules:
  0.0 42.6 jit_solution(12737697546968635904)
XLA Ops:
  0.0 41.3 %mixed_kernel.1 = (bf16[97,128,128]{2,1,0:T(8,128)(2,1)S(1)}, bf16[64,128,512]{2,1,0:T(8,128)(2,1)S(1)}, bf16[64,128,128]{2,1,0:T(8,128)(2,1)S(1)}, s32[64]{0:T(128)S(4)}, s32[64]{0:T(128)S(4)}, /*index=5*/s32[8]{0:T(128)S(4)}) custom-call(bf16[4096,128]{1,0:T(8,128)(2,1)} %z_ref.1, bf16[32,128,384]{2,1,0:T(8,128)(2,1)} %band_ref.1, ...), custom_call_target="tpu_custom_call" | custom-call | tf_op jit(solution)/shard_map/mixed_kernel/pallas_call | solution.py:455
  41.3 1.3 %impute_kernel.1 = bf16[64,128,128]{2,1,0:T(8,128)(2,1)} custom-call(s32[64]{0:T(128)S(4)} %get-tuple-element.11.start_ref, s32[64]{0:T(128)S(4)} %get-tuple-element.12.count_ref, s32[8]{0:T(128)S(4)} %get-tuple-element.13.touched, bf16[97,128,128]{2,1,0:T(8,128)(2,1)S(1)} %get-tuple-element.14.ext_ref, bf16[64,128,512]{2,1,0:T(8,128)(2,1)S(1)} %get-tuple-element.15.ld_ref, ...), custom_call_target="tpu_custom_call" | custom-call | tf_op jit(solution)/shard_map/impute_kernel/pallas_call | solution.py:521

commit v6 on v5

--- a/solution.py
+++ b/solution.py
@@ -290,7 +290,7 @@
         )
         return copy
 
-    at_end = has_left & (g == var_size - 1)
+    at_end = has_left & ((g == var_size - 1) | (g == var_size + 1))
     held = []
 
     def send_halos(c, which):

time: 42.9 us -> 44.1 us (1.028)
  the two profiles are of different devices: /device:TPU:0 before, /device:TPU:1 now
where the time goes in v6:
time: 44.1 us; the launch traced here: 43.9 us
  Pallas kernels  43.9 us (100%)
    pallas_call x1, Pallas kernels, mixed_with_neighbours(): pl.pallas_call(functools.partial(mixed_kernel, jobs, blocks, groups, var_...  41.8 us
    pallas_call x1, Pallas kernels, impute(): pl.pallas_call(functools.partial(impute_kernel, blocks, var_size), in_spe...  2.09 us

profile of v6, /device:TPU:1, one launch (start us, length us, event | category | flops | bytes accessed | tf_op | source)
XLA Modules:
  0.0 43.9 jit_solution(2973236703636099769)
XLA Ops:
  0.0 41.8 %mixed_kernel.1 = (bf16[97,128,128]{2,1,0:T(8,128)(2,1)S(1)}, bf16[64,128,512]{2,1,0:T(8,128)(2,1)S(1)}, bf16[64,128,128]{2,1,0:T(8,128)(2,1)S(1)}, s32[64]{0:T(128)S(4)}, s32[64]{0:T(128)S(4)}, /*index=5*/s32[8]{0:T(128)S(4)}) custom-call(bf16[4096,128]{1,0:T(8,128)(2,1)} %z_ref.1, bf16[32,128,384]{2,1,0:T(8,128)(2,1)} %band_ref.1, ...), custom_call_target="tpu_custom_call" | custom-call | tf_op jit(solution)/shard_map/mixed_kernel/pallas_call | solution.py:455
  41.9 2.1 %impute_kernel.1 = bf16[64,128,128]{2,1,0:T(8,128)(2,1)} custom-call(s32[64]{0:T(128)S(4)} %get-tuple-element.11.start_ref, s32[64]{0:T(128)S(4)} %get-tuple-element.12.count_ref, s32[8]{0:T(128)S(4)} %get-tuple-element.13.touched, bf16[97,128,128]{2,1,0:T(8,128)(2,1)S(1)} %get-tuple-element.14.ext_ref, bf16[64,128,512]{2,1,0:T(8,128)(2,1)S(1)} %get-tuple-element.15.ld_ref, ...), custom_call_target="tpu_custom_call" | custom-call | tf_op jit(solution)/shard_map/impute_kernel/pallas_call | solution.py:521
